TPU v7x, 1024 devices: a whole 4x4x32 slice. The times are simulated.
1024 devices in a mesh: expert: 8 (over y, core), tensor: 32 (over z), dp: 4 (over x).
Axes of the slice: x: 4, y: 4, z: 32, core: 2. Of those that a mesh axis runs over, the one named last changes fastest.
Arguments:
- tokens: bfloat16 [1024, 4096], P(('expert', 'dp'), 'tensor'), may hold values from -6 to 6
- grad_out: bfloat16 [1024, 4096], P(('expert', 'dp'), 'tensor'), may hold values from -6 to 6
- route_weights: float32 [1024, 2], P(('expert', 'dp')), may hold values from 0.1 to 0.9
- expert_ids: int32 [1024, 2], P(('expert', 'dp')), may hold values from 0 to 7, all different within a row; in each aligned block of 32 rows (0 to 31, 32 to 63, ...) at most 16 rows name the same one
- w_gate: bfloat16 [8, 4096, 8192], P('expert', None, 'tensor'), may hold values from -0.1875 to 0.1875
- w_up: bfloat16 [8, 4096, 8192], P('expert', None, 'tensor'), may hold values from -0.09375 to 0.09375
- w_down: bfloat16 [8, 4096, 8192], P('expert', None, 'tensor'), may hold values from -0.09375 to 0.09375
Outputs:
- grad_tokens: float32 [1024, 4096], P(('expert', 'dp'), 'tensor')
- grad_gate: bfloat16 [8, 4096, 8192], P('expert', 'dp', 'tensor')
- grad_up: bfloat16 [8, 4096, 8192], P('expert', 'dp', 'tensor')
Inputs may be any that keep to these rules, and one draw needn't show every extreme that they name: `expert_ids`: each row names 2 different experts. In each token block of 32 rows no expert is named by more than 16 rows, a bound that some block reaches.
All inputs are finite; a program needn't handle non-finite values.
Results may differ from a plain program's by a relative error of at most 0.009.
Values may be sent and summed in bfloat16 or wider, within the bound.
A program may use at most 32 MiB of HBM per device.

v0:
```python
import jax
import jax.numpy as jnp
from jax import lax
from jax.sharding import PartitionSpec as P


def slot_picker(expert_ids, n_experts, capacity):
    flat_ids = expert_ids.reshape(-1)
    expert_range = jnp.arange(n_experts, dtype=jnp.int32)
    onehot = (flat_ids[:, None] == expert_range[None, :]).astype(jnp.int32)
    earlier = jnp.cumsum(onehot, axis=0) - onehot
    position = jnp.sum(earlier * onehot, axis=1)
    slot_range = jnp.arange(capacity, dtype=jnp.int32)
    chosen = (flat_ids[None, None, :] == expert_range[:, None, None]) & (
        position[None, None, :] == slot_range[None, :, None]
    )
    return chosen.reshape(n_experts * capacity, flat_ids.shape[0])


def body(tokens, grad_out, route_weights, expert_ids, w_gate, w_up, w_down):
    n_experts = lax.axis_size("expert")
    tok_rows, top_count = expert_ids.shape
    capacity = tok_rows * top_count * 2 // n_experts
    chosen = slot_picker(expert_ids, n_experts, capacity)
    pick_send = jnp.where(chosen, 1.0, 0.0).astype(jnp.bfloat16)
    pick_back = jnp.transpose(jnp.where(chosen, 1.0, 0.0).astype(jnp.float32))
    weight_column = route_weights.reshape(-1, 1)
    x_copies = jnp.repeat(tokens, top_count, axis=0)
    dy_copies = jnp.repeat(grad_out, top_count, axis=0)
    scaled = (weight_column * dy_copies.astype(jnp.float32)).astype(jnp.bfloat16)
    sent_x = jnp.dot(pick_send, x_copies, preferred_element_type=jnp.float32).astype(jnp.bfloat16)
    sent_dy = jnp.dot(pick_send, scaled, preferred_element_type=jnp.float32).astype(jnp.bfloat16)
    sent_x, sent_dy = (
        sent_x.reshape(n_experts, capacity, -1),
        sent_dy.reshape(n_experts, capacity, -1),
    )
    got_x, got_dy = (
        lax.all_to_all(sent_x, "expert", split_axis=0, concat_axis=0, tiled=True),
        lax.all_to_all(sent_dy, "expert", split_axis=0, concat_axis=0, tiled=True),
    )
    rows_x, rows_dy = (
        lax.all_gather(got_x.reshape(n_experts * capacity, -1), "tensor", axis=1, tiled=True),
        lax.all_gather(got_dy.reshape(n_experts * capacity, -1), "tensor", axis=1, tiled=True),
    )
    gate_w = w_gate[0]
    up_w = w_up[0]
    down_w = w_down[0]
    gate_pre = jnp.dot(rows_x, gate_w, preferred_element_type=jnp.float32)
    up_pre = jnp.dot(rows_x, up_w, preferred_element_type=jnp.float32)
    sigmoid_gate = jax.nn.sigmoid(gate_pre)
    activated = gate_pre * sigmoid_gate
    d_hidden = jnp.dot(rows_dy, down_w, preferred_element_type=jnp.float32)
    d_up = (d_hidden * activated).astype(jnp.bfloat16)
    d_gate = (d_hidden * up_pre * sigmoid_gate * (1.0 + gate_pre * (1.0 - sigmoid_gate))).astype(
        jnp.bfloat16
    )
    dims_inner = (((1,), (1,)), ((), ()))
    partial_x = lax.dot_general(d_gate, gate_w, dims_inner, preferred_element_type=jnp.float32)
    partial_x = partial_x + lax.dot_general(
        d_up, up_w, dims_inner, preferred_element_type=jnp.float32
    )
    shares = lax.psum_scatter(partial_x, "tensor", scatter_dimension=1, tiled=True)
    returned = lax.all_to_all(
        shares.reshape(n_experts, capacity, -1), "expert", split_axis=0, concat_axis=0, tiled=True
    )
    per_assign = jnp.dot(
        pick_back,
        returned.reshape(n_experts * capacity, -1),
        precision=lax.Precision.HIGHEST,
        preferred_element_type=jnp.float32,
    )
    grad_tokens = per_assign.reshape(tok_rows, top_count, -1).sum(axis=1)
    hidden_width = gate_w.shape[1]
    dims_outer = (((0,), (0,)), ((), ()))
    gate_part = lax.dot_general(rows_x, d_gate, dims_outer, preferred_element_type=jnp.float32)
    up_part = lax.dot_general(rows_x, d_up, dims_outer, preferred_element_type=jnp.float32)
    summed = lax.psum_scatter(
        jnp.concatenate([gate_part, up_part], axis=1).astype(jnp.bfloat16),
        "dp",
        scatter_dimension=0,
        tiled=True,
    ).astype(jnp.float32)
    grad_g = summed[:, :hidden_width]
    grad_u = summed[:, hidden_width:]
    return (grad_tokens, grad_g.astype(jnp.bfloat16)[None], grad_u.astype(jnp.bfloat16)[None])


def solution(mesh):
    placed = (
        P(("expert", "dp"), "tensor"),
        P(("expert", "dp"), "tensor"),
        P(("expert", "dp"), None),
        P(("expert", "dp"), None),
        P("expert", None, "tensor"),
        P("expert", None, "tensor"),
        P("expert", None, "tensor"),
    )
    return jax.shard_map(
        body,
        mesh=mesh,
        in_specs=placed,
        out_specs=(
            P(("expert", "dp"), "tensor"),
            P("expert", "dp", "tensor"),
            P("expert", "dp", "tensor"),
        ),
        check_vma=False,
    )
```

profile of v0, /device:TPU:1, one launch (start us, length us, event | category | flops | bytes accessed | tf_op | source)
XLA Modules:
  0.0 498.2 jit_solution(6904163819245736596)
XLA Ops:
  7.2 0.0 copy-start
  7.2 0.0 all-gather.5.cloned.1.call-start
  7.2 0.9 copy.19
  8.1 0.1 eq.51
  8.2 0.1 fusion.22
  8.3 0.1 reduce_window_sum.11
  8.4 0.2 select_reduce_fusion
  8.6 0.7 broadcast_in_dim.29
  9.4 0.1 convolution_convert_fusion.2
  9.5 21.9 %all_to_all.15 = bf16[8,16,128]{2,1,0:T(8,128)(2,1)} all-to-all(bf16[8,16,128]{2,1,0:T(8,128)(2,1)S(1)} %bitcast.64), channel_id=1, replica_groups=mesh['expert'=8,'tensor'=32,'dp'=4] {'expert'}, dimensions={0} | all-to-all | bytes 65536 | tf_op jit(solution)/shard_map/all_to_all | solution.py:38
  31.4 0.0 all-gather.5.cloned.1.call-update
  31.4 0.0 all-gather.3.cloned.1.call-start
  31.4 0.7 convert_element_type.55
  32.1 0.8 copy.21
  32.9 0.1 multiply_convert_fusion.1
  33.0 0.1 convolution_convert_fusion.3
  33.1 8.5 %all_to_all.16 = bf16[8,16,128]{2,1,0:T(8,128)(2,1)} all-to-all(bf16[8,16,128]{2,1,0:T(8,128)(2,1)S(1)} %bitcast.63), channel_id=1, replica_groups=mesh['expert'=8,'tensor'=32,'dp'=4] {'expert'}, dimensions={0} | all-to-all | bytes 65536 | tf_op jit(solution)/shard_map/all_to_all | solution.py:39
  41.6 0.0 all-gather.3.cloned.1.call-update
  41.6 0.0 reduce-scatter.3.cloned.1.call-start
  41.7 95.3 %all-gather.5.cloned.1.call-done = bf16[128,4096]{1,0:T(8,128)(2,1)} async-done(((bf16[128,128]{1,0:T(8,128)(2,1)}), bf16[128,4096]{1,0:T(8,128)(2,1)}) %all-gather.5.cloned.1.call-update) | async-done | bytes 1048592 | tf_op jit(solution)/shard_map/all_gather | solution.py:42
  137.0 0.0 copy-done
  137.0 1.7 fusion.2
  138.6 0.0 copy-start.1
  138.7 126.6 %all-gather.3.cloned.1.call-done = bf16[128,4096]{1,0:T(8,128)(2,1)} async-done(((bf16[128,128]{1,0:T(8,128)(2,1)}), bf16[128,4096]{1,0:T(8,128)(2,1)}) %all-gather.3.cloned.1.call-update) | async-done | bytes 1048592 | tf_op jit(solution)/shard_map/all_gather | solution.py:43
  265.3 0.0 copy-start.2
  265.3 2.5 multiply_convert_fusion
  267.8 0.0 copy-done.1
  267.8 0.0 copy-done.2
  267.8 0.5 fusion.18
  268.3 0.8 fusion
  269.1 2.1 convolution_add_fusion
  271.2 0.0 reduce-scatter.3.cloned.1.call-update
  271.3 0.0 reduce-scatter.5.cloned.1.call-start
  271.3 0.7 convolution_convert_fusion
  272.1 0.7 convolution_convert_fusion.1
  272.8 2.4 pad_maximum_fusion
  275.3 0.0 reduce-scatter.5.cloned.1.call-update
  275.3 127.4 %reduce-scatter.3.cloned.1.call-done = f32[128,128]{1,0:T(8,128)} async-done(((f32[128,4096]{1,0:T(8,128)}), f32[128,128]{1,0:T(8,128)}) %reduce-scatter.3.cloned.1.call-update) | async-done | bytes 65552 | tf_op jit(solution)/shard_map/reduce_scatter | solution.py:62
  402.7 26.9 %all-to-all-start.2 = ((f32[8,16,128]{2,1,0:T(8,128)}), f32[8,16,128]{2,1,0:T(8,128)S(1)}, u32[]{:S(2)}, u32[]{:S(2)}) async-start(f32[8,16,128]{2,1,0:T(8,128)} %bitcast.67), calls=%async_computation.3 | async-start | bytes 131072 | tf_op jit(solution)/shard_map/all_to_all | solution.py:63
  429.6 0.1 copy.20
  429.6 4.8 all-to-all-done.2
  434.4 0.8 convolution_reduce_fusion
  435.2 53.2 %reduce-scatter.5.cloned.1.call-done = bf16[1024,512]{0,1:T(8,128)(2,1)} async-done(((bf16[4096,512]{0,1:T(8,128)(2,1)}), bf16[1024,512]{0,1:T(8,128)(2,1)}) %reduce-scatter.5.cloned.1.call-update) | async-done | bytes 1048592 | tf_op jit(solution)/shard_map/reduce_scatter | solution.py:77
  488.4 1.3 slice_bitcast_fusion
  489.7 1.0 copy.23
  490.7 1.0 copy.24
  (3 shorter events, 0.0 us)
Async XLA Ops:
  7.2 129.8 %copy-start = (bf16[1,4096,256]{2,1,0:T(8,128)(2,1)S(1)}, bf16[1,4096,256]{2,1,0:T(8,128)(2,1)}, u32[]{:S(2)}) copy-start(bf16[1,4096,256]{2,1,0:T(8,128)(2,1)} %param.11) | copy-start | bytes 6291460
  7.2 129.8 %all-gather.5.cloned.1.call-start = ((), (), s32[]{:S(2)}) async-start(), calls=%async_computation.6 | async-start | bytes 1081344 | tf_op jit(solution)/shard_map/all_gather | solution.py:42
  31.4 233.9 %all-gather.3.cloned.1.call-start = ((), (), s32[]{:S(2)}) async-start(), calls=%async_computation.5 | async-start | bytes 1081344 | tf_op jit(solution)/shard_map/all_gather | solution.py:43
  41.6 361.0 %reduce-scatter.3.cloned.1.call-start = ((), (), s32[]{:S(2)}) async-start(), calls=%async_computation.7 | async-start | bytes 2162688 | tf_op jit(solution)/shard_map/reduce_scatter | solution.py:62
  138.6 129.1 %copy-start.1 = (bf16[128,4096]{1,0:T(8,128)(2,1)S(1)}, bf16[128,4096]{1,0:T(8,128)(2,1)}, u32[]{:S(2)}) copy-start(bf16[128,4096]{1,0:T(8,128)(2,1)} %all-gather.5.cloned.1.call-done) | copy-start | bytes 3145732
  265.3 2.5 copy-start.2
  271.3 217.1 %reduce-scatter.5.cloned.1.call-start = ((), (), s32[]{:S(2)}) async-start(), calls=%async_computation.8 | async-start | bytes 5242880 | tf_op jit(solution)/shard_map/reduce_scatter | solution.py:77
  402.7 31.8 %all-to-all-start.2 = ((f32[8,16,128]{2,1,0:T(8,128)}), f32[8,16,128]{2,1,0:T(8,128)S(1)}, u32[]{:S(2)}, u32[]{:S(2)}) async-start(f32[8,16,128]{2,1,0:T(8,128)} %bitcast.67), calls=%async_computation.3 | async-start | bytes 131072 | tf_op jit(solution)/shard_map/all_to_all | solution.py:63
Sparse Core Ops, SparseCore 0:
  31.5 105.4 all-gather.4
  139.6 125.6 all-gather.2
  271.4 131.2 reduce-scatter.2
  405.9 82.4 reduce-scatter.4
where the time goes:
time: 499 us; the launch traced here: 498 us
  waiting for transfers between devices  407 us (82%)
  blocking collectives  30.4 us (6%)
  starting transfers between devices  27.1 us (5%)
  between operations  13.9 us (3%)
  matrix products  10.1 us (2%)
  local copies, waits for them, and re-layouts  5.83 us (1%)
    reduce_scatter x1, waiting for transfers between devices, body(): lax.psum_scatter(partial_x, 'tensor', scatter_dimension=1, tiled=True)  127 us
    all_gather x1, waiting for transfers between devices, body(): lax.all_gather(got_dy.reshape(n_experts * capacity, -1), 'tensor', axis=1...  127 us
    all_gather x1, waiting for transfers between devices, body(): lax.all_gather(got_x.reshape(n_experts * capacity, -1), 'tensor', axis=1,...  95.3 us
    reduce_scatter x1, waiting for transfers between devices, body(): lax.psum_scatter(jnp.concatenate([gate_part, up_part], axis=1).astype(jnp...  53.2 us
    all_to_all x1, starting transfers between devices, body(): lax.all_to_all(shares.reshape(n_experts, capacity, -1), 'expert', split_a...  26.9 us
    all_to_all x1, blocking collectives, body(): lax.all_to_all(sent_x, 'expert', split_axis=0, concat_axis=0, tiled=True)  21.9 us
  transfers between devices with their start and end apart: 5, of which 5 were waited for; matrix products, arithmetic and copies ran while one was open for 2% of the time, Pallas kernels for 0%

commit v1 on v0

v1 whole, which is shorter than its diff:
```python
import functools

import jax
import jax.numpy as jnp
from jax import lax
from jax.experimental import pallas as pl
from jax.experimental.pallas import tpu as pltpu
from jax.sharding import PartitionSpec as P

STRIDE = 2
LINK = jnp.bfloat16
F32 = jnp.float32
BF16 = jnp.bfloat16
NT = (((1,), (1,)), ((), ()))
TN = (((0,), (0,)), ((), ()))


def remote(src, dst, send_sem, recv_sem, **where):
    return pltpu.make_async_remote_copy(
        src_ref=src,
        dst_ref=dst,
        send_sem=send_sem,
        recv_sem=recv_sem,
        device_id=where,
        device_id_type=pl.DeviceIdType.MESH,
    )


def kernel(
    sizes,
    tok_ref, dy_ref, ids_ref, rw_ref, wg_hbm, wu_hbm, wd_hbm,
    gt_ref, gg_hbm, gu_hbm,
    wg, wu, wd, agp, agm, dsp, rows, acc_g, acc_u, acc_d, dd, ddall, xall,
    cs, cr, sbuf, rr, own, gg, gu,
    w_sem, ag_ssem, ag_rsem, ds_sem, dr_sem, xs_sem, xr_sem, dds_sem, ddr_sem,
    cs_sem, cr_sem, rs_sem, rr_sem, out_sem,
):
    n_e, n_z, n_x, cap = sizes
    S = STRIDE
    H = n_z // 2
    K = H // S
    toks = tok_ref.shape[0]
    feat = tok_ref.shape[1]
    ff = wg.shape[1]
    n_rows = n_e * cap
    per_q = n_z // n_x
    me = lax.axis_index("expert")
    z = lax.axis_index("tensor")
    mq = lax.axis_index("dp")

    loads = [
        pltpu.make_async_copy(src.at[0], dst, w_sem.at[i])
        for i, (src, dst) in enumerate(((wg_hbm, wg), (wu_hbm, wu), (wd_hbm, wd)))
    ]
    for load in loads:
        load.start()

    barrier = pltpu.get_barrier_semaphore()
    partners = []
    for m in range(1, S + 1):
        partners.append({"tensor": lax.rem(z + m, n_z)})
        partners.append({"tensor": lax.rem(z + n_z - m, n_z)})
    for i in range(1, n_e):
        partners.append({"expert": lax.rem(me + i, n_e)})
    for i in range(1, n_x):
        partners.append({"dp": lax.rem(mq + i, n_x)})
    for where in partners:
        pl.semaphore_signal(barrier, inc=1, device_id=where, device_id_type=pl.DeviceIdType.MESH)

    agm[0, :, 0:feat] = tok_ref[...]
    agm[0, :, feat : 2 * feat] = dy_ref[...]

    row = lax.broadcasted_iota(jnp.int32, (n_rows, toks), 0)
    row_expert = row // cap
    row_slot = (row - row_expert * cap).astype(F32)
    first = ids_ref[0:1, :] == row_expert
    second = ids_ref[1:2, :] == row_expert
    named = jnp.where(first, 1.0, jnp.where(second, 1.0, 0.0)).astype(F32)
    before = lax.broadcasted_iota(jnp.int32, (toks, toks), 0)
    after = lax.broadcasted_iota(jnp.int32, (toks, toks), 1)
    earlier = jnp.where(before < after, 1.0, 0.0).astype(BF16)
    place = jnp.dot(named.astype(BF16), earlier, preferred_element_type=F32)
    pick_f = jnp.where(place == row_slot, named, 0.0)
    weight = jnp.where(first, rw_ref[0:1, :], rw_ref[1:2, :])
    p_col = jnp.sum(pick_f * weight, axis=1, keepdims=True)
    pick = pick_f.astype(BF16)
    eye = jnp.where(before == after, 1.0, 0.0).astype(BF16)
    pick_back = lax.dot_general(eye, pick, NT, preferred_element_type=F32).astype(BF16)

    pl.semaphore_wait(barrier, len(partners))

    def up(m):
        return lax.rem(z + m, n_z)

    def down(m):
        return lax.rem(z + n_z - m, n_z)

    sends = []

    def ag_copy(sign, j, m):
        dist = S * j + m
        if sign > 0:
            src = agm.at[0] if j == 0 else agp.at[S * j - 1]
            return remote(src, agp.at[dist - 1], ag_ssem.at[0, dist - 1], ag_rsem.at[0, dist - 1], tensor=up(m))
        return remote(agm.at[S * j], agm.at[dist], ag_ssem.at[1, dist], ag_rsem.at[1, dist], tensor=down(m))

    def ag_wait(sign, dist):
        if sign > 0:
            remote(agp.at[dist - 1], agp.at[dist - 1], ag_ssem.at[0, dist - 1], ag_rsem.at[0, dist - 1], tensor=up(1)).wait_recv()
        elif dist > 0:
            remote(agm.at[dist], agm.at[dist], ag_ssem.at[1, dist], ag_rsem.at[1, dist], tensor=up(1)).wait_recv()

    def batch_of(sign, j):
        return j if sign > 0 else K + j

    def dists_of(sign, j):
        return [S * j + s + (1 if sign > 0 else 0) for s in range(S)]

    me_rows = pl.ds(pl.multiple_of(me * cap, cap), cap)

    def exchange(src, dst, b, send_sem, recv_sem):
        for i in range(1, n_e):
            e = lax.rem(me + i, n_e)
            copy = remote(
                src.at[b, :, pl.ds(pl.multiple_of(e * cap, cap), cap), :],
                dst.at[b, :, me_rows, :],
                send_sem.at[b], recv_sem.at[b], expert=e,
            )
            copy.start()
        dst[b, :, me_rows, :] = src[b, :, me_rows, :]

    def exchange_desc(src, dst, b, send_sem, recv_sem):
        part = pl.ds(0, n_rows - cap)
        return remote(src.at[b, :, part, :], dst.at[b, :, part, :], send_sem.at[b], recv_sem.at[b],
                      expert=lax.rem(me + 1, n_e))

    def dispatch(sign, j):
        b = batch_of(sign, j)
        refs = []
        for dist in dists_of(sign, j):
            if not (sign > 0 and dist % S == 0) and not (sign < 0 and dist % S == 0):
                ag_wait(sign, dist)
            refs.append(agp[dist - 1] if sign > 0 else agm[dist])
        wide = jnp.concatenate(refs, axis=1)
        picked = jnp.dot(pick, wide, preferred_element_type=F32)
        for s in range(S):
            base = 2 * feat * s
            dsp[b, s, :, 0:feat] = picked[:, base : base + feat].astype(BF16)
            dsp[b, s, :, feat : 2 * feat] = (picked[:, base + feat : base + 2 * feat] * p_col).astype(BF16)
        exchange(dsp, rows, b, ds_sem, dr_sem)

    started = []

    def consume(sign, j):
        b = batch_of(sign, j)
        exchange_desc(dsp, rows, b, ds_sem, dr_sem).wait_recv()
        if not started:
            for load in loads:
                load.wait()
        places = [down(dist) if sign > 0 else up(dist) for dist in dists_of(sign, j)]
        x = jnp.concatenate([rows[b, s, :, 0:feat] for s in range(S)], axis=1)
        d = jnp.concatenate([rows[b, s, :, feat : 2 * feat] for s in range(S)], axis=1)

        def slab(w):
            return jnp.concatenate(
                [w[pl.ds(pl.multiple_of(at * feat, feat), feat), :] for at in places], axis=0)

        for lhs, w, acc in ((x, wg, acc_g), (x, wu, acc_u), (d, wd, acc_d)):
            term = jnp.dot(lhs, slab(w), preferred_element_type=F32)
            acc[...] = term if not started else acc[...] + term
        started.append(True)
        for s, at in enumerate(places):
            to = at // per_q
            local = lax.rem(at, per_q)

            @pl.when(to == mq)
            def _():
                xall[mq, local] = rows[b, s, :, 0:feat]

            if n_x > 1:
                @pl.when(to != mq)
                def _():
                    remote(rows.at[b, s, :, pl.ds(0, feat)], xall.at[mq, local], xs_sem.at[0],
                           xr_sem.at[mq], dp=to).start()

    for j in range(K):
        if j:
            ag_wait(1, S * j)
        for m in [S] + list(range(1, S)):
            copy = ag_copy(1, j, m)
            copy.start()
            sends.append(copy)
        if j:
            ag_wait(-1, S * j)
        for m in [S] + list(range(1, S)):
            if S * j + m < H:
                copy = ag_copy(-1, j, m)
                copy.start()
                sends.append(copy)
        if j >= 1:
            dispatch(1, j - 1)
            dispatch(-1, j - 1)
        if j >= 2:
            consume(1, j - 2)
            consume(-1, j - 2)
    dispatch(-1, K - 1)
    ag_wait(1, H)
    dispatch(1, K - 1)
    if K >= 2:
        consume(1, K - 2)
        consume(-1, K - 2)
    consume(-1, K - 1)
    consume(1, K - 1)

    gate_pre = acc_g[...]
    up_pre = acc_u[...]
    d_hidden = acc_d[...]
    sig = jax.nn.sigmoid(gate_pre)
    d_up = (d_hidden * (gate_pre * sig)).astype(BF16)
    d_gate = (d_hidden * up_pre * sig * (1.0 + gate_pre * (1.0 - sig))).astype(BF16)
    dd[:, 0:ff] = d_gate
    dd[:, ff : 2 * ff] = d_up
    ddall[mq] = dd[...]

    def contribute(sign, j):
        b = batch_of(sign, j)
        places = [up(dist) if sign > 0 else down(dist) for dist in dists_of(sign, j)]

        def slab(w):
            return jnp.concatenate(
                [w[pl.ds(pl.multiple_of(at * feat, feat), feat), :] for at in places], axis=0)

        part = lax.dot_general(dd[:, 0:ff], slab(wg), NT, preferred_element_type=F32)
        part = part + lax.dot_general(dd[:, ff : 2 * ff], slab(wu), NT, preferred_element_type=F32)
        for s in range(S):
            cs[b, s] = part[:, feat * s : feat * (s + 1)].astype(BF16)
        exchange(cs, cr, b, cs_sem, cr_sem)

    def ring_copy(sign, j, m):
        where = (up if sign > 0 else down)(S if m == 0 else m)
        d = 0 if sign > 0 else 1
        return remote(sbuf.at[d, j, m], rr.at[d, j, m], rs_sem.at[d, j, m], rr_sem.at[d, j, m], tensor=where)

    def combine(sign, j):
        b = batch_of(sign, j)
        d = 0 if sign > 0 else 1
        exchange_desc(cs, cr, b, cs_sem, cr_sem).wait_recv()
        wide = jnp.concatenate([cr[b, s] for s in range(S)], axis=1)
        comb = jnp.dot(pick_back, wide, preferred_element_type=F32)
        for s in range(S):
            piece = comb[:, feat * s : feat * (s + 1)]
            l = (s + 1) % S if sign > 0 else s
            if l == 0:
                own[d, j] = piece
            else:
                sbuf[d, j, l] = piece.astype(LINK)
                copy = ring_copy(sign, j, l)
                copy.start()
                sends.append(copy)

    def relay_sum(sign, j):
        d = 0 if sign > 0 else 1
        total = None
        if sign > 0 and j > 0:
            total = own[0, j - 1]
        elif sign < 0:
            total = own[1, j]
        if j < K:
            for l in range(1, S):
                ring_copy(sign, j, l).wait_recv()
                piece = rr[d, j, l].astype(F32)
                total = piece if total is None else total + piece
            if sign > 0 or j < K - 1:
                ring_copy(sign, j, 0).wait_recv()
                piece = rr[d, j, 0].astype(F32)
                total = piece if total is None else total + piece
        return total

    def relay(sign, j):
        d = 0 if sign > 0 else 1
        total = relay_sum(sign, j)
        sbuf[d, j - 1, 0] = total.astype(LINK)
        copy = ring_copy(sign, j - 1, 0)
        copy.start()
        sends.append(copy)

    def dd_desc(q):
        return remote(ddall.at[q], ddall.at[q], dds_sem.at[0], ddr_sem.at[q], dp=lax.rem(mq + 1, n_x))

    contribute(1, K - 1)
    contribute(-1, K - 1)
    for i in range(1, n_x):
        remote(ddall.at[mq], ddall.at[mq], dds_sem.at[0], ddr_sem.at[mq], dp=lax.rem(mq + i, n_x)).start()
    if K >= 2:
        contribute(1, K - 2)
        contribute(-1, K - 2)
    combine(1, K - 1)
    combine(-1, K - 1)

    state = {"slot": 0, "ready": False}

    def grads(count):
        if not state["ready"]:
            state["ready"] = True
            for i in range(1, n_x):
                q = lax.rem(mq + i, n_x)
                remote(xall.at[q], xall.at[q], xs_sem.at[0], xr_sem.at[q], dp=lax.rem(mq + 1, n_x)).wait_recv()
                dd_desc(q).wait_recv()
        for s in range(state["slot"], min(state["slot"] + count, per_q)):
            lhs = jnp.concatenate([xall[q, s] for q in range(n_x)], axis=0)
            rhs = jnp.concatenate([ddall[q] for q in range(n_x)], axis=0)
            out = lax.dot_general(lhs, rhs, TN, preferred_element_type=F32)
            gg[feat * s : feat * (s + 1), :] = out[:, 0:ff].astype(BF16)
            gu[feat * s : feat * (s + 1), :] = out[:, ff : 2 * ff].astype(BF16)
        state["slot"] = min(state["slot"] + count, per_q)

    late = max(1, K // 2)
    for j in range(K - 1, -1, -1):
        relay(1, j + 1)
        if j + 1 <= K - 1:
            relay(-1, j + 1)
        if j >= 1:
            combine(1, j - 1)
            combine(-1, j - 1)
        if j >= 2:
            contribute(1, j - 2)
            contribute(-1, j - 2)
        if j < late:
            grads(-(-per_q // late))
    outs = [
        pltpu.make_async_copy(gg, gg_hbm.at[0], out_sem.at[0]),
        pltpu.make_async_copy(gu, gu_hbm.at[0], out_sem.at[1]),
    ]
    for copy in outs:
        copy.start()
    gt_ref[...] = relay_sum(1, 0) + relay_sum(-1, 0)

    for copy in sends:
        copy.wait_send()
    for b in range(2 * K):
        exchange_desc(dsp, rows, b, ds_sem, dr_sem).wait_send()
        exchange_desc(cs, cr, b, cs_sem, cr_sem).wait_send()
    if n_x > 1:
        part = pl.ds(0, n_x - 1)
        remote(xall.at[part], xall.at[part], xs_sem.at[0], xr_sem.at[0], dp=lax.rem(mq + 1, n_x)).wait_send()
        remote(ddall.at[part], ddall.at[part], dds_sem.at[0], ddr_sem.at[0], dp=lax.rem(mq + 1, n_x)).wait_send()
    for copy in outs:
        copy.wait()


def body(tokens, grad_out, route_weights, expert_ids, w_gate, w_up, w_down):
    n_e, n_z, n_x = lax.axis_size("expert"), lax.axis_size("tensor"), lax.axis_size("dp")
    toks, feat = tokens.shape
    ff = w_gate.shape[2]
    width = w_gate.shape[1]
    cap = toks * expert_ids.shape[1] * 2 // n_e
    n_rows = n_e * cap
    S = STRIDE
    H = n_z // 2
    K = H // S
    per_q = n_z // n_x
    vmem = pl.BlockSpec(memory_space=pltpu.VMEM)
    hbm = pl.BlockSpec(memory_space=pl.ANY)
    dma = pltpu.SemaphoreType.DMA
    return pl.pallas_call(
        functools.partial(kernel, (n_e, n_z, n_x, cap)),
        name="moe_backward",
        out_shape=(
            jax.ShapeDtypeStruct((toks, feat), F32),
            jax.ShapeDtypeStruct((1, width // n_x, ff), BF16),
            jax.ShapeDtypeStruct((1, width // n_x, ff), BF16),
        ),
        in_specs=[vmem] * 4 + [hbm] * 3,
        out_specs=(vmem, hbm, hbm),
        scratch_shapes=[
            pltpu.VMEM((width, ff), BF16),
            pltpu.VMEM((width, ff), BF16),
            pltpu.VMEM((width, ff), BF16),
            pltpu.VMEM((H, toks, 2 * feat), BF16),
            pltpu.VMEM((H, toks, 2 * feat), BF16),
            pltpu.VMEM((2 * K, S, n_rows, 2 * feat), BF16),
            pltpu.VMEM((2 * K, S, n_rows, 2 * feat), BF16),
            pltpu.VMEM((n_rows, ff), F32),
            pltpu.VMEM((n_rows, ff), F32),
            pltpu.VMEM((n_rows, ff), F32),
            pltpu.VMEM((n_rows, 2 * ff), BF16),
            pltpu.VMEM((n_x, n_rows, 2 * ff), BF16),
            pltpu.VMEM((n_x, per_q, n_rows, feat), BF16),
            pltpu.VMEM((2 * K, S, n_rows, feat), BF16),
            pltpu.VMEM((2 * K, S, n_rows, feat), BF16),
            pltpu.VMEM((2, K, S, toks, feat), LINK),
            pltpu.VMEM((2, K, S, toks, feat), LINK),
            pltpu.VMEM((2, K, toks, feat), F32),
            pltpu.VMEM((width // n_x, ff), BF16),
            pltpu.VMEM((width // n_x, ff), BF16),
            dma((3,)),
            dma((2, H)), dma((2, H)),
            dma((2 * K,)), dma((2 * K,)),
            dma((1,)), dma((n_x,)),
            dma((1,)), dma((n_x,)),
            dma((2 * K,)), dma((2 * K,)),
            dma((2, K, S)), dma((2, K, S)),
            dma((2,)),
        ],
        compiler_params=pltpu.CompilerParams(collective_id=0, has_side_effects=True),
    )(tokens, grad_out, expert_ids.T, route_weights.T, w_gate, w_up, w_down)


def solution(mesh):
    placed = (
        P(("expert", "dp"), "tensor"),
        P(("expert", "dp"), "tensor"),
        P(("expert", "dp"), None),
        P(("expert", "dp"), None),
        P("expert", None, "tensor"),
        P("expert", None, "tensor"),
        P("expert", None, "tensor"),
    )
    return jax.shard_map(
        body,
        mesh=mesh,
        in_specs=placed,
        out_specs=(
            P(("expert", "dp"), "tensor"),
            P("expert", "dp", "tensor"),
            P("expert", "dp", "tensor"),
        ),
        check_vma=False,
    )
```

time: 499 us -> 101 us (0.20)
  waiting for transfers between devices: 407 us -> 0 us
  Pallas kernels: 0 us -> 95 us
  blocking collectives: 30.4 us -> 0 us
  starting transfers between devices: 27.1 us -> 0 us
  between operations: 13.9 us -> 0.64 us
  matrix products: 10.1 us -> 0 us
    all_gather x2 -> x0, waiting for transfers between devices: 222 us -> none  [the longest x1 127 us: body(): lax.all_gather(got_dy.reshape(n_experts * capacity, -1), 'tensor', axis=1...]
    reduce_scatter x2 -> x0, waiting for transfers between devices: 181 us -> none  [the longest x1 127 us: body(): lax.psum_scatter(partial_x, 'tensor', scatter_dimension=1, tiled=True)]
    pallas_call x0 -> x1, Pallas kernels: none -> 95 us  [body(): pl.pallas_call(functools.partial(kernel, (n_e, n_z, n_x, cap)), name='moe...]
    all_to_all x2 -> x0, blocking collectives: 30.4 us -> none  [the longest x1 21.9 us: body(): lax.all_to_all(sent_x, 'expert', split_axis=0, concat_axis=0, tiled=True)]
    all_to_all x1 -> x0, starting transfers between devices: 26.9 us -> none  [body(): lax.all_to_all(shares.reshape(n_experts, capacity, -1), 'expert', split_a...]
    dot_general x10 -> x0, matrix products: 10.1 us -> none  [the longest x1 2.5 us: body(): d_hidden = jnp.dot(rows_dy, down_w, preferred_element_type=jnp.float32)]
  transfers between devices with their start and end apart: 5 -> 0, of which waited for: 5 -> 0; matrix products, arithmetic and copies ran while one was open for 2% -> 0% of each run, Pallas kernels for 0% -> 0%
where the time goes in v1:
time: 101 us
  Pallas kernels  95 us (94%)
  local copies, waits for them, and re-layouts  5.06 us (5%)
    pallas_call x1, Pallas kernels, body(): pl.pallas_call(functools.partial(kernel, (n_e, n_z, n_x, cap)), name='moe...  95 us
    unnamed x3, local copies, waits for them, and re-layouts  5.06 us

profile of v1, /device:TPU:1, one launch (start us, length us, event | category | flops | bytes accessed | tf_op | source)
XLA Modules:
  0.0 100.7 jit_solution(2280107567461191096)
XLA Ops:
  0.6 95.0 %moe_backward.1 = (f32[32,128]{1,0:T(8,128)}, bf16[1,1024,256]{2,1,0:T(8,128)(2,1)}, bf16[1,1024,256]{2,1,0:T(8,128)(2,1)}) custom-call(bf16[32,128]{1,0:T(8,128)(2,1)} %tok_ref.1, bf16[32,128]{1,0:T(8,128)(2,1)} %dy_ref.1, s32[2,32]{1,0:T(2,128)} %bitcast.2, f32[2,32]{1,0:T(2,128)} %bitcast.3, bf16[1,4096,256]{2,1,0:T(8,128)(2,1)} %wg_hbm.1, ...), custom_call_target="tpu_custom_call" | custom-call | tf_op jit(solution)/shard_map/moe_backward/pallas_call | solution.py:365
  95.6 1.3 %copy.13 = f32[32,128]{1,0:T(8,128)} copy(f32[32,128]{1,0:T(8,128)} %get-tuple-element.6) | data formatting | bytes 32768
  97.0 1.9 %copy.14 = bf16[1,1024,256]{2,1,0:T(8,128)(2,1)} copy(bf16[1,1024,256]{2,1,0:T(8,128)(2,1)} %get-tuple-element.7) | data formatting | bytes 1048576
  98.8 1.9 %copy.15 = bf16[1,1024,256]{2,1,0:T(8,128)(2,1)} copy(bf16[1,1024,256]{2,1,0:T(8,128)(2,1)} %get-tuple-element.8) | data formatting | bytes 1048576

commit v2 on v1

v2 whole, which is shorter than its diff:
```python
import functools

import jax
import jax.numpy as jnp
from jax import lax
from jax.experimental import pallas as pl
from jax.experimental.pallas import tpu as pltpu
from jax.sharding import PartitionSpec as P

STRIDE = 4
LINK = jnp.bfloat16
F32 = jnp.float32
BF16 = jnp.bfloat16
NT = (((1,), (1,)), ((), ()))
TN = (((0,), (0,)), ((), ()))


def remote(src, dst, send_sem, recv_sem, **where):
    return pltpu.make_async_remote_copy(
        src_ref=src,
        dst_ref=dst,
        send_sem=send_sem,
        recv_sem=recv_sem,
        device_id=where,
        device_id_type=pl.DeviceIdType.MESH,
    )


def kernel(
    sizes,
    tok_hbm, dy_hbm, ids_hbm, rw_hbm, wg_hbm, wu_hbm, wd_hbm,
    gt_ref, gg, gu,
    tok_ref, dy_ref, ids_ref, rw_ref, wg, wu, wd, agp, agm, dsp, rows, acc_g, acc_u, acc_d, dd, ddall, xall,
    cs, cr, sbuf, rr, own,
    in_sem, w_sem, ag_ssem, ag_rsem, ds_sem, dr_sem, xs_sem, xr_sem, dds_sem, ddr_sem,
    cs_sem, cr_sem, rs_sem, rr_sem,
):
    n_e, n_z, n_x, cap = sizes
    S = STRIDE
    H = n_z // 2
    K = H // S
    toks = tok_hbm.shape[0]
    feat = tok_hbm.shape[1]
    ff = wg.shape[1]
    n_rows = n_e * cap
    per_q = n_z // n_x
    me = lax.axis_index("expert")
    z = lax.axis_index("tensor")
    mq = lax.axis_index("dp")

    firsts = [
        pltpu.make_async_copy(src, dst, in_sem.at[i])
        for i, (src, dst) in enumerate(((tok_hbm, tok_ref), (dy_hbm, dy_ref), (ids_hbm, ids_ref), (rw_hbm, rw_ref)))
    ]
    for load in firsts:
        load.start()
    loads = [
        pltpu.make_async_copy(src.at[0], dst, w_sem.at[i])
        for i, (src, dst) in enumerate(((wg_hbm, wg), (wu_hbm, wu), (wd_hbm, wd)))
    ]
    for load in loads:
        load.start()

    barrier = pltpu.get_barrier_semaphore()
    partners = []
    for m in range(1, S + 1):
        partners.append({"tensor": lax.rem(z + m, n_z)})
        partners.append({"tensor": lax.rem(z + n_z - m, n_z)})
    for i in range(1, n_e):
        partners.append({"expert": lax.rem(me + i, n_e)})
    for i in range(1, n_x):
        partners.append({"dp": lax.rem(mq + i, n_x)})
    for where in partners:
        pl.semaphore_signal(barrier, inc=1, device_id=where, device_id_type=pl.DeviceIdType.MESH)

    for load in firsts[:2]:
        load.wait()
    agm[0, :, 0:feat] = tok_ref[...]
    agm[0, :, feat : 2 * feat] = dy_ref[...]

    pl.semaphore_wait(barrier, len(partners))

    def up(m):
        return lax.rem(z + m, n_z)

    def down(m):
        return lax.rem(z + n_z - m, n_z)

    sends = []

    def ag_copy(sign, j, m):
        dist = S * j + m
        if sign > 0:
            src = agm.at[0] if j == 0 else agp.at[S * j - 1]
            return remote(src, agp.at[dist - 1], ag_ssem.at[0, dist - 1], ag_rsem.at[0, dist - 1], tensor=up(m))
        return remote(agm.at[S * j], agm.at[dist], ag_ssem.at[1, dist], ag_rsem.at[1, dist], tensor=down(m))

    def ag_wait(sign, dist):
        if sign > 0:
            remote(agp.at[dist - 1], agp.at[dist - 1], ag_ssem.at[0, dist - 1], ag_rsem.at[0, dist - 1], tensor=up(1)).wait_recv()
        elif dist > 0:
            remote(agm.at[dist], agm.at[dist], ag_ssem.at[1, dist], ag_rsem.at[1, dist], tensor=up(1)).wait_recv()

    def span(sign, part, j):
        if part:
            first, count = S * j + 1, S - 1
        else:
            first, count = (S * (j + 1) if sign > 0 else S * j), 1
        at = first - 1 if sign > 0 else H + first
        return first, count, at, (0 if sign > 0 else 2 * K) + 2 * j + part

    def dists_of(sign, part, j):
        first, count, _, _ = span(sign, part, j)
        return list(range(first, first + count))

    me_rows = pl.ds(pl.multiple_of(me * cap, cap), cap)

    def exchange(src, dst, group, send_sem, recv_sem):
        _, count, at, g = group
        held = pl.ds(at, count)
        for i in range(1, n_e):
            e = lax.rem(me + i, n_e)
            copy = remote(
                src.at[held, pl.ds(pl.multiple_of(e * cap, cap), cap), :],
                dst.at[held, me_rows, :],
                send_sem.at[g], recv_sem.at[g], expert=e,
            )
            copy.start()
        dst[at : at + count, me_rows, :] = src[at : at + count, me_rows, :]

    def exchange_desc(src, dst, group, send_sem, recv_sem):
        _, count, at, g = group
        held, part = pl.ds(at, count), pl.ds(0, n_rows - cap)
        return remote(src.at[held, part, :], dst.at[held, part, :], send_sem.at[g], recv_sem.at[g],
                      expert=lax.rem(me + 1, n_e))

    handed = {S * j + S - 1 for j in range(K - 1)} if S > 2 else set()

    def hand_copy(sign, dist):
        at = slot(sign, dist)[2]
        return remote(rows.at[slot(sign, dist - 1)[2]], rows.at[at], ds_sem.at[at], dr_sem.at[at],
                      tensor=(up if sign > 0 else down)(1))

    arrived = set()

    def await_rows(sign, dist):
        if (sign, dist) in arrived:
            return
        arrived.add((sign, dist))
        if dist in handed:
            hand_copy(sign, dist).wait_recv()
        else:
            exchange_desc(dsp, rows, slot(sign, dist), ds_sem, dr_sem).wait_recv()

    def hand(sign, dist):
        await_rows(sign, dist - 1)
        copy = hand_copy(sign, dist)
        copy.start()
        sends.append(copy)

    def slot(sign, dist):
        at = dist - 1 if sign > 0 else H + dist
        return dist, 1, at, at

    def dispatch(sign, dist):
        group = slot(sign, dist)
        at = group[2]
        picked = jnp.dot(pick, agp[dist - 1] if sign > 0 else agm[dist], preferred_element_type=F32)
        dsp[at, :, 0:feat] = picked[:, 0:feat].astype(BF16)
        dsp[at, :, feat : 2 * feat] = (picked[:, feat : 2 * feat] * p_col).astype(BF16)
        exchange(dsp, rows, group, ds_sem, dr_sem)

    started = []

    def consume(sign, j):
        parts = (1, 0) if sign > 0 else (0, 1)
        dists = [dist for part in parts for dist in dists_of(sign, part, j)]
        for dist in dists:
            await_rows(sign, dist)
        at0 = slot(sign, dists[0])[2]
        if not started:
            for load in loads:
                load.wait()
        places = [down(dist) if sign > 0 else up(dist) for dist in dists]
        x = jnp.concatenate([rows[at0 + s, :, 0:feat] for s in range(S)], axis=1)
        d = jnp.concatenate([rows[at0 + s, :, feat : 2 * feat] for s in range(S)], axis=1)

        def slab(w):
            return jnp.concatenate(
                [w[pl.ds(pl.multiple_of(at * feat, feat), feat), :] for at in places], axis=0)

        for lhs, w, acc in ((x, wg, acc_g), (x, wu, acc_u), (d, wd, acc_d)):
            term = jnp.dot(lhs, slab(w), preferred_element_type=F32)
            acc[...] = term if not started else acc[...] + term
        started.append(True)
        for s, at in enumerate(places):
            to = at // per_q
            local = lax.rem(at, per_q)

            @pl.when(to == mq)
            def _():
                xall[mq, local] = rows[at0 + s, :, 0:feat]

            if n_x > 1:
                @pl.when(to != mq)
                def _():
                    remote(rows.at[at0 + s, :, pl.ds(0, feat)], xall.at[mq, local], xs_sem.at[0],
                           xr_sem.at[mq], dp=to).start()

    def ag_send(sign, j, m):
        if sign > 0 or S * j + m < H:
            copy = ag_copy(sign, j, m)
            copy.start()
            sends.append(copy)

    def ag_step(j):
        for sign in (1, -1):
            if j:
                ag_wait(sign, S * j)
            ag_send(sign, j, S)
        for m in range(1, S):
            for sign in (1, -1):
                if S * j + m not in handed:
                    ag_send(sign, j, m)

    def spread(j):
        if j:
            dispatch(1, S * j)
        dispatch(-1, S * j)
        for m in range(1, S):
            for sign in (1, -1):
                if S * j + m not in handed:
                    ag_wait(sign, S * j + m)
                    dispatch(sign, S * j + m)
        if j and S * j - 1 in handed:
            for sign in (1, -1):
                hand(sign, S * j - 1)

    ag_step(0)
    for load in firsts[2:]:
        load.wait()
    row = lax.broadcasted_iota(jnp.int32, (n_rows, toks), 0)
    row_expert = row // cap
    row_slot = (row - row_expert * cap).astype(F32)
    first = ids_ref[0:1, :] == row_expert
    second = ids_ref[1:2, :] == row_expert
    named = jnp.where(first, 1.0, jnp.where(second, 1.0, 0.0)).astype(F32)
    before = lax.broadcasted_iota(jnp.int32, (toks, toks), 0)
    after = lax.broadcasted_iota(jnp.int32, (toks, toks), 1)
    earlier = jnp.where(before < after, 1.0, 0.0).astype(BF16)
    place = jnp.dot(named.astype(BF16), earlier, preferred_element_type=F32)
    pick_f = jnp.where(place == row_slot, named, 0.0)
    weight = jnp.where(first, rw_ref[0:1, :], rw_ref[1:2, :])
    p_col = jnp.sum(pick_f * weight, axis=1, keepdims=True)
    pick = pick_f.astype(BF16)
    eye = jnp.where(before == after, 1.0, 0.0).astype(BF16)
    pick_back = lax.dot_general(eye, pick, NT, preferred_element_type=F32).astype(BF16)

    spread(0)
    for j in range(1, K):
        ag_step(j)
        spread(j)
    for j in range(K // 2):
        consume(-1, j)
        consume(1, j)
    ag_wait(1, H)
    dispatch(1, H)
    for j in range(K // 2, K):
        consume(-1, j)
        consume(1, j)

    gate_pre = acc_g[...]
    up_pre = acc_u[...]
    d_hidden = acc_d[...]
    sig = jax.nn.sigmoid(gate_pre)
    d_up = (d_hidden * (gate_pre * sig)).astype(BF16)
    d_gate = (d_hidden * up_pre * sig * (1.0 + gate_pre * (1.0 - sig))).astype(BF16)
    dd[:, 0:ff] = d_gate
    dd[:, ff : 2 * ff] = d_up
    ddall[mq] = dd[...]

    def contribute(sign, part, j):
        group = span(sign, part, j)
        _, count, at, _ = group
        places = [up(dist) if sign > 0 else down(dist) for dist in dists_of(sign, part, j)]

        def slab(w):
            slabs = [w[pl.ds(pl.multiple_of(to * feat, feat), feat), :] for to in places]
            return jnp.concatenate(slabs, axis=0) if count > 1 else slabs[0]

        term = lax.dot_general(dd[:, 0:ff], slab(wg), NT, preferred_element_type=F32)
        term = term + lax.dot_general(dd[:, ff : 2 * ff], slab(wu), NT, preferred_element_type=F32)
        for s in range(count):
            cs[at + s] = term[:, feat * s : feat * (s + 1)].astype(BF16)
        exchange(cs, cr, group, cs_sem, cr_sem)

    def ring_copy(sign, j, m):
        where = (up if sign > 0 else down)(S if m == 0 else m)
        d = 0 if sign > 0 else 1
        return remote(sbuf.at[d, j, m], rr.at[d, j, m], rs_sem.at[d, j, m], rr_sem.at[d, j, m], tensor=where)

    def combine(sign, part, j):
        group = span(sign, part, j)
        _, count, at, _ = group
        d = 0 if sign > 0 else 1
        exchange_desc(cs, cr, group, cs_sem, cr_sem).wait_recv()
        wide = jnp.concatenate([cr[at + s] for s in range(count)], axis=1) if count > 1 else cr[at]
        comb = jnp.dot(pick_back, wide, preferred_element_type=F32)
        if not part:
            own[d, j] = comb
            return
        for s in range(count):
            sbuf[d, j, s + 1] = comb[:, feat * s : feat * (s + 1)].astype(LINK)
            copy = ring_copy(sign, j, s + 1)
            copy.start()
            sends.append(copy)

    def relay_sum(sign, j):
        d = 0 if sign > 0 else 1
        total = None
        if sign > 0 and j > 0:
            total = own[0, j - 1]
        elif sign < 0:
            total = own[1, j]
        if j < K:
            for l in range(1, S):
                ring_copy(sign, j, l).wait_recv()
                piece = rr[d, j, l].astype(F32)
                total = piece if total is None else total + piece
            if sign > 0 or j < K - 1:
                ring_copy(sign, j, 0).wait_recv()
                piece = rr[d, j, 0].astype(F32)
                total = piece if total is None else total + piece
        return total

    def relay(sign, j):
        d = 0 if sign > 0 else 1
        total = relay_sum(sign, j)
        sbuf[d, j - 1, 0] = total.astype(LINK)
        copy = ring_copy(sign, j - 1, 0)
        copy.start()
        sends.append(copy)

    def dd_desc(q):
        return remote(ddall.at[q], ddall.at[q], dds_sem.at[0], ddr_sem.at[q], dp=lax.rem(mq + 1, n_x))

    state = {"slot": 0, "ready": False}

    def grads(count):
        if not state["ready"]:
            state["ready"] = True
            for i in range(1, n_x):
                q = lax.rem(mq + i, n_x)
                remote(xall.at[q], xall.at[q], xs_sem.at[0], xr_sem.at[q], dp=lax.rem(mq + 1, n_x)).wait_recv()
                dd_desc(q).wait_recv()
        for s in range(state["slot"], min(state["slot"] + count, per_q)):
            lhs = jnp.concatenate([xall[q, s] for q in range(n_x)], axis=0)
            rhs = jnp.concatenate([ddall[q] for q in range(n_x)], axis=0)
            out = lax.dot_general(lhs, rhs, TN, preferred_element_type=F32)
            gg[0, feat * s : feat * (s + 1), :] = out[:, 0:ff].astype(BF16)
            gu[0, feat * s : feat * (s + 1), :] = out[:, ff : 2 * ff].astype(BF16)
        state["slot"] = min(state["slot"] + count, per_q)

    def give(j):
        contribute(1, 1, j)
        contribute(-1, 1, j)
        contribute(-1, 0, j)
        if j:
            contribute(1, 0, j - 1)

    def take(j):
        combine(1, 1, j)
        combine(-1, 1, j)
        combine(-1, 0, j)
        if j:
            combine(1, 0, j - 1)

    contribute(1, 0, K - 1)
    give(K - 1)
    for i in range(1, n_x):
        remote(ddall.at[mq], ddall.at[mq], dds_sem.at[0], ddr_sem.at[mq], dp=lax.rem(mq + i, n_x)).start()
    for j in range(K - 2, max(K - 4, -1), -1):
        give(j)
    combine(1, 0, K - 1)
    relay(1, K)
    take(K - 1)
    for j in range(K - 4, -1, -1):
        give(j)
    for j in range(K - 2, -1, -1):
        take(j)
        relay(1, j + 1)
        relay(-1, j + 1)
    grads(per_q)
    gt_ref[...] = relay_sum(1, 0) + relay_sum(-1, 0)

    for copy in sends:
        copy.wait_send()
    for sign in (1, -1):
        for part in (0, 1):
            for j in range(K):
                for dist in dists_of(sign, part, j):
                    if dist not in handed:
                        exchange_desc(dsp, rows, slot(sign, dist), ds_sem, dr_sem).wait_send()
                exchange_desc(cs, cr, span(sign, part, j), cs_sem, cr_sem).wait_send()
    if n_x > 1:
        part = pl.ds(0, n_x - 1)
        remote(xall.at[part], xall.at[part], xs_sem.at[0], xr_sem.at[0], dp=lax.rem(mq + 1, n_x)).wait_send()
        remote(ddall.at[part], ddall.at[part], dds_sem.at[0], ddr_sem.at[0], dp=lax.rem(mq + 1, n_x)).wait_send()


def body(tokens, grad_out, route_weights, expert_ids, w_gate, w_up, w_down):
    n_e, n_z, n_x = lax.axis_size("expert"), lax.axis_size("tensor"), lax.axis_size("dp")
    toks, feat = tokens.shape
    ff = w_gate.shape[2]
    width = w_gate.shape[1]
    cap = toks * expert_ids.shape[1] * 2 // n_e
    n_rows = n_e * cap
    S = STRIDE
    H = n_z // 2
    K = H // S
    per_q = n_z // n_x
    inputs = (tokens, grad_out, expert_ids.T, route_weights.T, w_gate, w_up, w_down)
    vmem = pl.BlockSpec(memory_space=pltpu.VMEM)
    hbm = pl.BlockSpec(memory_space=pl.ANY)
    dma = pltpu.SemaphoreType.DMA
    return pl.pallas_call(
        functools.partial(kernel, (n_e, n_z, n_x, cap)),
        name="moe_backward",
        out_shape=(
            jax.ShapeDtypeStruct((toks, feat), F32),
            jax.ShapeDtypeStruct((1, width // n_x, ff), BF16),
            jax.ShapeDtypeStruct((1, width // n_x, ff), BF16),
        ),
        in_specs=[hbm] * 7,
        out_specs=(vmem, vmem, vmem),
        scratch_shapes=[
            pltpu.VMEM(tokens.shape, BF16),
            pltpu.VMEM(tokens.shape, BF16),
            pltpu.VMEM(expert_ids.shape[::-1], jnp.int32),
            pltpu.VMEM(expert_ids.shape[::-1], F32),
            pltpu.VMEM((width, ff), BF16),
            pltpu.VMEM((width, ff), BF16),
            pltpu.VMEM((width, ff), BF16),
            pltpu.VMEM((H, toks, 2 * feat), BF16),
            pltpu.VMEM((H, toks, 2 * feat), BF16),
            pltpu.VMEM((2 * H, n_rows, 2 * feat), BF16),
            pltpu.VMEM((2 * H, n_rows, 2 * feat), BF16),
            pltpu.VMEM((n_rows, ff), F32),
            pltpu.VMEM((n_rows, ff), F32),
            pltpu.VMEM((n_rows, ff), F32),
            pltpu.VMEM((n_rows, 2 * ff), BF16),
            pltpu.VMEM((n_x, n_rows, 2 * ff), BF16),
            pltpu.VMEM((n_x, per_q, n_rows, feat), BF16),
            pltpu.VMEM((2 * H, n_rows, feat), BF16),
            pltpu.VMEM((2 * H, n_rows, feat), BF16),
            pltpu.VMEM((2, K, S, toks, feat), LINK),
            pltpu.VMEM((2, K, S, toks, feat), LINK),
            pltpu.VMEM((2, K, toks, feat), F32),
            dma((4,)), dma((3,)),
            dma((2, H)), dma((2, H)),
            dma((2 * H,)), dma((2 * H,)),
            dma((1,)), dma((n_x,)),
            dma((1,)), dma((n_x,)),
            dma((4 * K,)), dma((4 * K,)),
            dma((2, K, S)), dma((2, K, S)),
        ],
        compiler_params=pltpu.CompilerParams(collective_id=0, has_side_effects=True, vmem_limit_bytes=30 * 2**20),
    )(*[pltpu.with_memory_space_constraint(a, pltpu.HBM) for a in inputs])


def solution(mesh):
    placed = (
        P(("expert", "dp"), "tensor"),
        P(("expert", "dp"), "tensor"),
        P(("expert", "dp"), None),
        P(("expert", "dp"), None),
        P("expert", None, "tensor"),
        P("expert", None, "tensor"),
        P("expert", None, "tensor"),
    )
    return jax.shard_map(
        body,
        mesh=mesh,
        in_specs=placed,
        out_specs=(
            P(("expert", "dp"), "tensor"),
            P("expert", "dp", "tensor"),
            P("expert", "dp", "tensor"),
        ),
        check_vma=False,
    )
```

time: 101 us -> 80.3 us (0.80); the launches traced: 101 us -> 78.9 us
  Pallas kernels: 95 us -> 76 us
  local copies, waits for them, and re-layouts: 5.06 us -> 2.19 us
    pallas_call x1, Pallas kernels: 95 us -> 76 us  [body(): pl.pallas_call(functools.partial(kernel, (n_e, n_z, n_x, cap)), name='moe...]
    unnamed x3, local copies, waits for them, and re-layouts: 5.06 us -> 2.19 us
where the time goes in v2:
time: 80.3 us; the launch traced here: 78.9 us
  Pallas kernels  76 us (95%)
  local copies, waits for them, and re-layouts  2.19 us (3%)
    pallas_call x1, Pallas kernels, body(): pl.pallas_call(functools.partial(kernel, (n_e, n_z, n_x, cap)), name='moe...  76 us
    unnamed x3, local copies, waits for them, and re-layouts  2.19 us

profile of v2, /device:TPU:1, one launch (start us, length us, event | category | flops | bytes accessed | tf_op | source)
XLA Modules:
  0.0 78.9 jit_solution(8930802845194194600)
XLA Ops:
  0.6 76.0 %moe_backward.1 = (f32[32,128]{1,0:T(8,128)S(1)}, bf16[1,1024,256]{2,1,0:T(8,128)(2,1)S(1)}, bf16[1,1024,256]{2,1,0:T(8,128)(2,1)S(1)}) custom-call(bf16[32,128]{1,0:T(8,128)(2,1)} %tok_hbm.1, bf16[32,128]{1,0:T(8,128)(2,1)} %dy_hbm.1, s32[2,32]{1,0:T(2,128)} %bitcast.2, f32[2,32]{1,0:T(2,128)} %bitcast.3, bf16[1,4096,256]{2,1,0:T(8,128)(2,1)} %wg_hbm.1, ...), custom_call_target="tpu_custom_call" | custom-call | tf_op jit(solution)/shard_map/moe_backward/pallas_call | solution.py:426
  76.7 0.6 copy.13
  77.3 0.8 %copy.14 = bf16[1,1024,256]{2,1,0:T(8,128)(2,1)} copy(bf16[1,1024,256]{2,1,0:T(8,128)(2,1)S(1)} %get-tuple-element.7) | data formatting | bytes 1048576
  78.1 0.8 %copy.15 = bf16[1,1024,256]{2,1,0:T(8,128)(2,1)} copy(bf16[1,1024,256]{2,1,0:T(8,128)(2,1)S(1)} %get-tuple-element.8) | data formatting | bytes 1048576

commit v3 on v2

--- a/solution.py
+++ b/solution.py
@@ -29,11 +29,11 @@
 def kernel(
     sizes,
     tok_hbm, dy_hbm, ids_hbm, rw_hbm, wg_hbm, wu_hbm, wd_hbm,
-    gt_ref, gg, gu,
+    gt_ref, gg_out, gu_out,
     tok_ref, dy_ref, ids_ref, rw_ref, wg, wu, wd, agp, agm, dsp, rows, acc_g, acc_u, acc_d, dd, ddall, xall,
-    cs, cr, sbuf, rr, own,
+    cs, cr, sbuf, rr, own, gg, gu,
     in_sem, w_sem, ag_ssem, ag_rsem, ds_sem, dr_sem, xs_sem, xr_sem, dds_sem, ddr_sem,
-    cs_sem, cr_sem, rs_sem, rr_sem,
+    cs_sem, cr_sem, rs_sem, rr_sem, out_sem,
 ):
     n_e, n_z, n_x, cap = sizes
     S = STRIDE
@@ -86,20 +86,18 @@
     def down(m):
         return lax.rem(z + n_z - m, n_z)
 
-    sends = []
-
     def ag_copy(sign, j, m):
         dist = S * j + m
         if sign > 0:
             src = agm.at[0] if j == 0 else agp.at[S * j - 1]
-            return remote(src, agp.at[dist - 1], ag_ssem.at[0, dist - 1], ag_rsem.at[0, dist - 1], tensor=up(m))
-        return remote(agm.at[S * j], agm.at[dist], ag_ssem.at[1, dist], ag_rsem.at[1, dist], tensor=down(m))
+            return remote(src, agp.at[dist - 1], ag_ssem.at[0], ag_rsem.at[0, dist - 1], tensor=up(m))
+        return remote(agm.at[S * j], agm.at[dist], ag_ssem.at[0], ag_rsem.at[1, dist], tensor=down(m))
 
     def ag_wait(sign, dist):
         if sign > 0:
-            remote(agp.at[dist - 1], agp.at[dist - 1], ag_ssem.at[0, dist - 1], ag_rsem.at[0, dist - 1], tensor=up(1)).wait_recv()
+            remote(agp.at[dist - 1], agp.at[dist - 1], ag_ssem.at[0], ag_rsem.at[0, dist - 1], tensor=up(1)).wait_recv()
         elif dist > 0:
-            remote(agm.at[dist], agm.at[dist], ag_ssem.at[1, dist], ag_rsem.at[1, dist], tensor=up(1)).wait_recv()
+            remote(agm.at[dist], agm.at[dist], ag_ssem.at[0], ag_rsem.at[1, dist], tensor=up(1)).wait_recv()
 
     def span(sign, part, j):
         if part:
@@ -123,7 +121,7 @@
             copy = remote(
                 src.at[held, pl.ds(pl.multiple_of(e * cap, cap), cap), :],
                 dst.at[held, me_rows, :],
-                send_sem.at[g], recv_sem.at[g], expert=e,
+                send_sem.at[0], recv_sem.at[g], expert=e,
             )
             copy.start()
         dst[at : at + count, me_rows, :] = src[at : at + count, me_rows, :]
@@ -131,14 +129,14 @@
     def exchange_desc(src, dst, group, send_sem, recv_sem):
         _, count, at, g = group
         held, part = pl.ds(at, count), pl.ds(0, n_rows - cap)
-        return remote(src.at[held, part, :], dst.at[held, part, :], send_sem.at[g], recv_sem.at[g],
+        return remote(src.at[held, part, :], dst.at[held, part, :], send_sem.at[0], recv_sem.at[g],
                       expert=lax.rem(me + 1, n_e))
 
     handed = {S * j + S - 1 for j in range(K - 1)} if S > 2 else set()
 
     def hand_copy(sign, dist):
         at = slot(sign, dist)[2]
-        return remote(rows.at[slot(sign, dist - 1)[2]], rows.at[at], ds_sem.at[at], dr_sem.at[at],
+        return remote(rows.at[slot(sign, dist - 1)[2]], rows.at[at], ds_sem.at[1], dr_sem.at[at],
                       tensor=(up if sign > 0 else down)(1))
 
     arrived = set()
@@ -156,7 +154,6 @@
         await_rows(sign, dist - 1)
         copy = hand_copy(sign, dist)
         copy.start()
-        sends.append(copy)
 
     def slot(sign, dist):
         at = dist - 1 if sign > 0 else H + dist
@@ -211,7 +208,6 @@
         if sign > 0 or S * j + m < H:
             copy = ag_copy(sign, j, m)
             copy.start()
-            sends.append(copy)
 
     def ag_step(j):
         for sign in (1, -1):
@@ -297,7 +293,7 @@
     def ring_copy(sign, j, m):
         where = (up if sign > 0 else down)(S if m == 0 else m)
         d = 0 if sign > 0 else 1
-        return remote(sbuf.at[d, j, m], rr.at[d, j, m], rs_sem.at[d, j, m], rr_sem.at[d, j, m], tensor=where)
+        return remote(sbuf.at[d, j, m], rr.at[d, j, m], rs_sem.at[0], rr_sem.at[d, j, m], tensor=where)
 
     def combine(sign, part, j):
         group = span(sign, part, j)
@@ -313,7 +309,6 @@
             sbuf[d, j, s + 1] = comb[:, feat * s : feat * (s + 1)].astype(LINK)
             copy = ring_copy(sign, j, s + 1)
             copy.start()
-            sends.append(copy)
 
     def relay_sum(sign, j):
         d = 0 if sign > 0 else 1
@@ -339,7 +334,6 @@
         sbuf[d, j - 1, 0] = total.astype(LINK)
         copy = ring_copy(sign, j - 1, 0)
         copy.start()
-        sends.append(copy)
 
     def dd_desc(q):
         return remote(ddall.at[q], ddall.at[q], dds_sem.at[0], ddr_sem.at[q], dp=lax.rem(mq + 1, n_x))
@@ -391,21 +385,31 @@
         relay(1, j + 1)
         relay(-1, j + 1)
     grads(per_q)
+    outs = [
+        pltpu.make_async_copy(gg, gg_out, out_sem.at[0]),
+        pltpu.make_async_copy(gu, gu_out, out_sem.at[1]),
+    ]
+    for copy in outs:
+        copy.start()
     gt_ref[...] = relay_sum(1, 0) + relay_sum(-1, 0)
 
-    for copy in sends:
-        copy.wait_send()
-    for sign in (1, -1):
-        for part in (0, 1):
-            for j in range(K):
-                for dist in dists_of(sign, part, j):
-                    if dist not in handed:
-                        exchange_desc(dsp, rows, slot(sign, dist), ds_sem, dr_sem).wait_send()
-                exchange_desc(cs, cr, span(sign, part, j), cs_sem, cr_sem).wait_send()
+    n_hand = 2 * len(handed)
+
+    def drain(ref, sem, other):
+        remote(ref, ref, sem, other, tensor=up(1)).wait_send()
+
+    drain(dsp.at[pl.ds(0, 2 * H - 1 - n_hand), pl.ds(0, toks), :], ag_ssem.at[0], ag_rsem.at[0, 0])
+    drain(dsp.at[pl.ds(0, 2 * H - n_hand), pl.ds(0, n_rows - cap), :], ds_sem.at[0], dr_sem.at[0])
+    if n_hand:
+        drain(dsp.at[pl.ds(0, n_hand), :, :], ds_sem.at[1], dr_sem.at[0])
+    drain(cs.at[pl.ds(0, 2 * H), pl.ds(0, n_rows - cap), :], cs_sem.at[0], cr_sem.at[0])
+    drain(cs.at[pl.ds(0, 2 * H - 1), pl.ds(0, toks), :], rs_sem.at[0], rr_sem.at[0, 0, 0])
     if n_x > 1:
         part = pl.ds(0, n_x - 1)
         remote(xall.at[part], xall.at[part], xs_sem.at[0], xr_sem.at[0], dp=lax.rem(mq + 1, n_x)).wait_send()
         remote(ddall.at[part], ddall.at[part], dds_sem.at[0], ddr_sem.at[0], dp=lax.rem(mq + 1, n_x)).wait_send()
+    for copy in outs:
+        copy.wait()
 
 
 def body(tokens, grad_out, route_weights, expert_ids, w_gate, w_up, w_down):
@@ -421,6 +425,7 @@
     per_q = n_z // n_x
     inputs = (tokens, grad_out, expert_ids.T, route_weights.T, w_gate, w_up, w_down)
     vmem = pl.BlockSpec(memory_space=pltpu.VMEM)
+    anywhere = pl.BlockSpec(memory_space=pl.ANY)
     hbm = pl.BlockSpec(memory_space=pl.ANY)
     dma = pltpu.SemaphoreType.DMA
     return pl.pallas_call(
@@ -432,7 +437,7 @@
             jax.ShapeDtypeStruct((1, width // n_x, ff), BF16),
         ),
         in_specs=[hbm] * 7,
-        out_specs=(vmem, vmem, vmem),
+        out_specs=(vmem, anywhere, anywhere),
         scratch_shapes=[
             pltpu.VMEM(tokens.shape, BF16),
             pltpu.VMEM(tokens.shape, BF16),
@@ -456,13 +461,16 @@
             pltpu.VMEM((2, K, S, toks, feat), LINK),
             pltpu.VMEM((2, K, S, toks, feat), LINK),
             pltpu.VMEM((2, K, toks, feat), F32),
+            pltpu.VMEM((1, width // n_x, ff), BF16),
+            pltpu.VMEM((1, width // n_x, ff), BF16),
             dma((4,)), dma((3,)),
-            dma((2, H)), dma((2, H)),
-            dma((2 * H,)), dma((2 * H,)),
+            dma((1,)), dma((2, H)),
+            dma((2,)), dma((2 * H,)),
             dma((1,)), dma((n_x,)),
             dma((1,)), dma((n_x,)),
-            dma((4 * K,)), dma((4 * K,)),
-            dma((2, K, S)), dma((2, K, S)),
+            dma((1,)), dma((4 * K,)),
+            dma((1,)), dma((2, K, S)),
+            dma((2,)),
         ],
         compiler_params=pltpu.CompilerParams(collective_id=0, has_side_effects=True, vmem_limit_bytes=30 * 2**20),
     )(*[pltpu.with_memory_space_constraint(a, pltpu.HBM) for a in inputs])

time: 80.3 us -> 79.2 us (0.986)
  Pallas kernels: 76 us -> 74.9 us
    pallas_call x1, Pallas kernels: 76 us -> 74.9 us  [body(): pl.pallas_call(functools.partial(kernel, (n_e, n_z, n_x, cap)), name='moe...]
where the time goes in v3:
time: 79.2 us; the launch traced here: 77.8 us
  Pallas kernels  74.9 us (95%)
  local copies, waits for them, and re-layouts  2.19 us (3%)
    pallas_call x1, Pallas kernels, body(): pl.pallas_call(functools.partial(kernel, (n_e, n_z, n_x, cap)), name='moe...  74.9 us
    unnamed x3, local copies, waits for them, and re-layouts  2.19 us

profile of v3, /device:TPU:1, one launch (start us, length us, event | category | flops | bytes accessed | tf_op | source)
XLA Modules:
  0.0 77.8 jit_solution(2148507834434361910)
XLA Ops:
  0.6 74.9 %moe_backward.1 = (f32[32,128]{1,0:T(8,128)S(1)}, bf16[1,1024,256]{2,1,0:T(8,128)(2,1)S(1)}, bf16[1,1024,256]{2,1,0:T(8,128)(2,1)S(1)}) custom-call(bf16[32,128]{1,0:T(8,128)(2,1)} %tok_hbm.1, bf16[32,128]{1,0:T(8,128)(2,1)} %dy_hbm.1, s32[2,32]{1,0:T(2,128)} %bitcast.2, f32[2,32]{1,0:T(2,128)} %bitcast.3, bf16[1,4096,256]{2,1,0:T(8,128)(2,1)} %wg_hbm.1, ...), custom_call_target="tpu_custom_call" | custom-call | tf_op jit(solution)/shard_map/moe_backward/pallas_call | solution.py:431
  75.6 0.6 copy.13
  76.2 0.8 %copy.14 = bf16[1,1024,256]{2,1,0:T(8,128)(2,1)} copy(bf16[1,1024,256]{2,1,0:T(8,128)(2,1)S(1)} %get-tuple-element.7) | data formatting | bytes 1048576
  77.0 0.8 %copy.15 = bf16[1,1024,256]{2,1,0:T(8,128)(2,1)} copy(bf16[1,1024,256]{2,1,0:T(8,128)(2,1)S(1)} %get-tuple-element.8) | data formatting | bytes 1048576
